TPU v7x, 32 devices: a whole 2x2x4 slice. The times are simulated.
32 devices in a mesh: shard: 4 (over y, core), replica: 8 (over z, x).
Axes of the slice: x: 2, y: 2, z: 4, core: 2. Of those that a mesh axis runs over, the one named last changes fastest.
Arguments:
- tokens: bfloat16 [8, 1024, 1024], P('replica', 'shard'), may hold values from -6 to 6
- cotangent: bfloat16 [8, 1024, 1024], P('replica', 'shard'), may hold values from -6 to 6
- lengths: int32 [8], P('replica'), may hold values from 256 to 1024, as said below
- block_order: int32 [8, 8], P('replica'), may hold values from 0 to 7, as said below
- norm1_gain: bfloat16 [1024], P('shard'), may hold values from 0.099609375 to 1.8984375
- query_weight: bfloat16 [1024, 2048], P('shard'), may hold values from -0.1875 to 0.1875
- key_weight: bfloat16 [1024, 1024], P('shard'), may hold values from -0.1875 to 0.1875
- value_weight: bfloat16 [1024, 1024], P('shard'), may hold values from -0.1875 to 0.1875
- output_weight: bfloat16 [2048, 1024], P('shard'), may hold values from -1.5 to 1.5
- query_gain: bfloat16 [128], P('shard'), may hold values from 0.099609375 to 1.8984375
- key_gain: bfloat16 [128], P('shard'), may hold values from 0.099609375 to 1.8984375
- norm2_gain: bfloat16 [1024], P('shard'), may hold values from 0.099609375 to 1.8984375
- gate_weight: bfloat16 [1024, 3072], P('shard'), may hold values from -0.1875 to 0.1875
- up_weight: bfloat16 [1024, 3072], P('shard'), may hold values from -0.1875 to 0.1875
- down_weight: bfloat16 [3072, 1024], P('shard'), may hold values from -0.109375 to 0.109375
Outputs:
- output: bfloat16 [8, 1024, 1024], P('replica', 'shard')
- input_grad: float32 [8, 1024, 1024], P('replica', 'shard')
- norm1_gain_grad: float32 [1024], P('shard')
- query_weight_grad: float32 [1024, 2048], P('shard')
- key_weight_grad: float32 [1024, 1024], P('shard')
- value_weight_grad: float32 [1024, 1024], P('shard')
- output_weight_grad: float32 [2048, 1024], P('shard')
- query_gain_grad: float32 [128], P('shard')
- key_gain_grad: float32 [128], P('shard')
- norm2_gain_grad: float32 [1024], P('shard')
- gate_weight_grad: float32 [1024, 3072], P('shard')
- up_weight_grad: float32 [1024, 3072], P('shard')
- down_weight_grad: float32 [3072, 1024], P('shard')
Inputs may be any that keep to these rules, and one draw needn't show every extreme that they name: `lengths`: in every group of 1 sequence one has 1024 valid tokens; valid tokens hold positions 0 to length - 1. `block_order`: each row is a permutation of 0 to 7 in which places 2j and 2j + 1 hold blocks that add up to 7.
All inputs are finite; a program needn't handle non-finite values.
Results may differ from a plain program's by a relative error of at most 0.013.
Values may be sent and summed in bfloat16 or wider, within the bound.
A program may use at most 256 MiB of HBM per device.

v0:
```python
import jax
import jax.numpy as jnp
from jax import lax
from jax.sharding import PartitionSpec as P

EPSILON = 1e-06
ROPE_BASE = 1000000.0
BF = jnp.bfloat16
F32 = jnp.float32


def rms_scale(values, gain_vec):
    return (
        values * lax.rsqrt(jnp.mean(values * values, axis=-1, keepdims=True) + EPSILON) * gain_vec
    )


def rotate_half(values, cosine, sine_table):
    middle = values.shape[-1] // 2
    turned = jnp.concatenate([-values[..., middle:], values[..., :middle]], axis=-1)
    return values * cosine + turned * sine_table


def rotary_tables(position, head_width):
    middle = head_width // 2
    exponent = jnp.arange(middle, dtype=F32) * 2.0 / head_width
    inverse = ROPE_BASE ** (-exponent)
    phases = position.astype(F32)[..., None] * inverse
    phases = jnp.concatenate([phases, phases], axis=-1)
    return (jnp.cos(phases), jnp.sin(phases))


def mm(a, b):
    return jnp.einsum("ri,io->ro", a, b, preferred_element_type=F32)


def mm_t(a, b):
    return jnp.einsum("ro,io->ri", a, b, preferred_element_type=F32)


def mm_w(a, b):
    return jnp.einsum("ri,ro->io", a, b, preferred_element_type=F32)


def gather_rows(v):
    return lax.all_gather(v, "shard", axis=0, tiled=True)


def scatter_rows(v):
    return lax.psum_scatter(v.astype(BF), "shard", scatter_dimension=0, tiled=True).astype(F32)


def to_columns(w):
    return lax.all_to_all(w, "shard", split_axis=1, concat_axis=0, tiled=True)


def to_rows(g):
    return lax.all_to_all(g, "shard", split_axis=0, concat_axis=1, tiled=True)


def shards(
    tokens,
    cotangent,
    lengths,
    block_order,
    norm1_gain,
    query_weight,
    key_weight,
    value_weight,
    output_weight,
    query_gain,
    key_gain,
    norm2_gain,
    gate_weight,
    up_weight,
    down_weight,
):
    shard_count = lax.axis_size("shard")
    row_count = tokens.shape[1]
    block_count = block_order.shape[1]
    slot_len = row_count * shard_count
    block_len = slot_len // block_count
    head_width = query_gain.shape[0] * shard_count
    score_scale = head_width ** (-0.5)
    gains = lax.all_gather(
        jnp.concatenate([norm1_gain, norm2_gain, query_gain, key_gain]), "shard", axis=0
    )
    wide = norm1_gain.shape[0]
    gain_one = gains[:, :wide].reshape(-1).astype(F32)
    gain_two = gains[:, wide : 2 * wide].reshape(-1).astype(F32)
    gain_query = gains[:, 2 * wide : 2 * wide + query_gain.shape[0]].reshape(-1).astype(F32)
    gain_key = gains[:, 2 * wide + query_gain.shape[0] :].reshape(-1).astype(F32)
    w_qkv = tuple((to_columns(w) for w in (query_weight, key_weight, value_weight)))
    w_gate, w_up = (to_columns(gate_weight), to_columns(up_weight))
    heads = w_qkv[0].shape[1] // head_width
    kvs = w_qkv[1].shape[1] // head_width
    per = heads // kvs
    offsets = jnp.arange(slot_len, dtype=jnp.int32)
    pos_all = (
        jnp.repeat(block_order[0], block_len, total_repeat_length=slot_len) * block_len
        + offsets % block_len
    )
    pos_local = lax.dynamic_slice_in_dim(pos_all, lax.axis_index("shard") * row_count, row_count)
    valid_rows = (pos_local < lengths[0]).astype(F32)[:, None]
    allowed = pos_all[None, None, None, :] <= pos_all[None, None, :, None]
    inputs = tokens[0].astype(F32)
    normed_f, norm_one_back = jax.vjp(rms_scale, inputs, gain_one)
    normed = gather_rows(normed_f.astype(BF))
    grad_result = cotangent[0].astype(F32) * valid_rows
    grad_branch = gather_rows(grad_result.astype(BF))
    query_raw = mm(normed, w_qkv[0]).reshape(slot_len, heads, head_width)
    key_raw = mm(normed, w_qkv[1]).reshape(slot_len, kvs, head_width)
    value = mm(normed, w_qkv[2]).astype(BF).reshape(slot_len, kvs, head_width)
    cosine, sine = rotary_tables(pos_all, head_width)
    cosine, sine = (cosine[:, None, :], sine[:, None, :])

    def turn(q, k, gq, gk):
        return (
            rotate_half(rms_scale(q, gq), cosine, sine),
            rotate_half(rms_scale(k, gk), cosine, sine),
        )

    turned, turn_back = jax.vjp(turn, query_raw, key_raw, gain_query, gain_key)
    query = turned[0].astype(BF).reshape(slot_len, kvs, per, head_width)
    key = turned[1].astype(BF)

    def scores_of():
        raw = jnp.einsum("rkgd,tkd->kgrt", query, key, preferred_element_type=F32) * score_scale
        return jnp.where(allowed, raw, -1e30)

    scores = scores_of()
    row_top = jnp.max(scores, axis=-1, keepdims=True)
    log_total = row_top + jnp.log(jnp.sum(jnp.exp(scores - row_top), axis=-1, keepdims=True))
    probs = jnp.exp(scores - log_total).astype(BF)
    mixed = jnp.einsum("kgrt,tkd->rkgd", probs, value, preferred_element_type=F32)
    mixed = mixed.reshape(slot_len, heads * head_width).astype(BF)
    hidden = inputs + scatter_rows(mm(mixed, output_weight))
    normed2_f, norm_two_back = jax.vjp(rms_scale, hidden, gain_two)
    normed2 = gather_rows(normed2_f.astype(BF))
    active_f, swish_back = jax.vjp(
        lambda a, b: jax.nn.silu(a) * b, mm(normed2, w_gate), mm(normed2, w_up)
    )
    active = active_f.astype(BF)
    output = (valid_rows * (hidden + scatter_rows(mm(active, down_weight)))).astype(BF)
    grad_gate_f, grad_up_f = swish_back(mm_t(grad_branch, down_weight))
    grad_gate, grad_up = (grad_gate_f.astype(BF), grad_up_f.astype(BF))
    grad_hidden_norm, grad_gain_two = norm_two_back(
        scatter_rows(mm_t(grad_gate, w_gate) + mm_t(grad_up, w_up))
    )
    grad_hidden = grad_result + grad_hidden_norm
    grad_mixed_in = gather_rows(grad_hidden.astype(BF))
    grad_mixed = mm_t(grad_mixed_in, output_weight).astype(BF)
    grad_mixed = grad_mixed.reshape(slot_len, kvs, per, head_width)
    probs_f = jnp.exp(scores_of() - log_total)
    grad_probs = jnp.einsum("rkgd,tkd->kgrt", grad_mixed, value, preferred_element_type=F32)
    grad_value = jnp.einsum(
        "kgrt,rkgd->tkd", probs_f.astype(BF), grad_mixed, preferred_element_type=F32
    )
    row_inner = jnp.sum(probs_f * grad_probs, axis=-1, keepdims=True)
    grad_scores = (probs_f * (grad_probs - row_inner)).astype(BF)
    grad_query = (
        jnp.einsum("kgrt,tkd->rkgd", grad_scores, key, preferred_element_type=F32) * score_scale
    )
    grad_key = (
        jnp.einsum("kgrt,rkgd->tkd", grad_scores, query, preferred_element_type=F32) * score_scale
    )
    grad_query_raw, grad_key_raw, grad_gain_query, grad_gain_key = turn_back(
        (grad_query.reshape(slot_len, heads, head_width), grad_key)
    )
    grad_query_b = grad_query_raw.reshape(slot_len, -1).astype(BF)
    grad_key_b = grad_key_raw.reshape(slot_len, -1).astype(BF)
    grad_value_b = grad_value.reshape(slot_len, -1).astype(BF)
    grad_normed = (
        mm_t(grad_query_b, w_qkv[0]) + mm_t(grad_key_b, w_qkv[1]) + mm_t(grad_value_b, w_qkv[2])
    )
    grad_inputs_norm, grad_gain_one = norm_one_back(scatter_rows(grad_normed))
    input_grad = grad_hidden + grad_inputs_norm

    def total(v):
        return lax.psum(v.astype(BF), "replica").astype(F32)

    grad_down = total(mm_w(active, grad_branch))
    grad_gate_w = to_rows(total(mm_w(normed2, grad_gate)).astype(BF)).astype(F32)
    grad_up_w = to_rows(total(mm_w(normed2, grad_up)).astype(BF)).astype(F32)
    grad_output_w = total(mm_w(mixed, grad_mixed_in))
    grad_query_w = to_rows(total(mm_w(normed, grad_query_b)).astype(BF)).astype(F32)
    grad_key_w = to_rows(total(mm_w(normed, grad_key_b)).astype(BF)).astype(F32)
    grad_value_w = to_rows(total(mm_w(normed, grad_value_b)).astype(BF)).astype(F32)
    small = jnp.concatenate([grad_gain_one, grad_gain_two, grad_gain_query, grad_gain_key])
    small = lax.psum(small, ("shard", "replica"))
    at = lax.axis_index("shard")
    hw = query_gain.shape[0]

    def own(start, size):
        return lax.dynamic_slice_in_dim(small, start + at * size, size)

    model = wide * shard_count
    return (
        output[None],
        input_grad[None],
        own(0, wide),
        grad_query_w,
        grad_key_w,
        grad_value_w,
        grad_output_w,
        own(2 * model, hw),
        own(2 * model + head_width, hw),
        own(model, wide),
        grad_gate_w,
        grad_up_w,
        grad_down,
    )


def solution(mesh):
    rows, mat, vec = (P("replica", "shard", None), P("shard", None), P("shard"))
    placed = (rows, rows, P("replica"), P("replica", None), vec, mat, mat, mat, mat)
    placed += (vec, vec, vec, mat, mat, mat)
    outs = (rows, rows, vec, mat, mat, mat, mat, vec, vec, vec, mat, mat, mat)
    return jax.shard_map(shards, mesh=mesh, in_specs=placed, out_specs=outs, check_vma=False)
```

profile of v0, /device:TPU:0, one launch (start us, length us, event | category | flops | bytes accessed | tf_op | source)
XLA Modules:
  0.0 764.7 jit_solution(12287463658765484522)
XLA Ops:
  11.5 8.5 %all-reduce.4 = bf16[2304]{0:T(1024)(128)(2,1)S(1)} all-reduce(bf16[2304]{0:T(1024)(128)(2,1)S(1)} %dynamic-update-slice.3), channel_id=2, replica_groups=mesh['shard'=4,'replica'=8] {'shard'}, use_global_device_ids=true, to_apply=%add.4 | all-reduce | flops 2304 | bytes 9216
  28.5 4.6 compare_select_fusion.1
  33.1 6.2 all-to-all-done.1
  39.3 4.1 all-to-all-start
  47.2 5.5 all-to-all-done
  52.7 4.3 all-to-all-start.2
  64.9 6.6 all-to-all-done.2
  86.3 3.7 exponential_reduce_fusion
  92.0 6.1 convolution_convert_fusion.8
  98.1 3.9 convolution_convert_fusion
  102.1 31.8 %reduce-scatter.5.cloned.1.call-done = bf16[256,1024]{1,0:T(8,128)(2,1)} async-done(((bf16[1024,1024]{1,0:T(8,128)(2,1)}), bf16[256,1024]{1,0:T(8,128)(2,1)}) %reduce-scatter.5.cloned.1.call-update) | async-done | bytes 524304 | tf_op jit(solution)/shard_map/reduce_scatter | solution.py:50
  139.8 4.3 all-to-all-start.3
  149.6 25.8 %all-to-all-done.3 = bf16[256,4,768]{0,2,1:T(8,128)(2,1)} async-done(((bf16[256,4,768]{0,2,1:T(8,128)(2,1)}), bf16[256,4,768]{0,2,1:T(8,128)(2,1)}, u32[]{:S(2)}, u32[]{:S(2)}) %all-to-all-start.3) | async-done | bytes 1572896 | tf_op jit(solution)/shard_map/all_to_all | solution.py:54
  175.4 4.4 all-to-all-start.4
  182.7 28.1 %all-to-all-done.4 = bf16[256,4,768]{0,2,1:T(8,128)(2,1)} async-done(((bf16[256,4,768]{0,2,1:T(8,128)(2,1)}), bf16[256,4,768]{0,2,1:T(8,128)(2,1)}, u32[]{:S(2)}, u32[]{:S(2)}) %all-to-all-start.4) | async-done | bytes 1572896 | tf_op jit(solution)/shard_map/all_to_all | solution.py:54
  213.4 5.6 fusion.63
  222.5 7.2 multiply_convert_fusion
  235.5 31.5 %reduce-scatter.9.cloned.1.call-done = bf16[256,1024]{1,0:T(8,128)(2,1)} async-done(((bf16[1024,1024]{1,0:T(8,128)(2,1)}), bf16[256,1024]{1,0:T(8,128)(2,1)}) %reduce-scatter.9.cloned.1.call-update) | async-done | bytes 524304 | tf_op jit(solution)/shard_map/reduce_scatter | solution.py:50
  271.8 5.2 convolution_convert_fusion.3
  283.1 11.0 %all-gather.12.cloned.1.call-done = bf16[1024,1024]{1,0:T(8,128)(2,1)} async-done(((bf16[256,1024]{1,0:T(8,128)(2,1)}), bf16[1024,1024]{1,0:T(8,128)(2,1)}) %all-gather.12.cloned.1.call-update) | async-done | bytes 2097168 | tf_op jit(solution)/shard_map/all_gather | solution.py:46
  297.2 8.5 %fusion.18 = bf16[2,128,1024]{2,1,0:T(8,128)(2,1)S(1)} fusion(bf16[1024,2,2,128]{0,3,2,1:T(8,128)(2,1)S(1)} %bitcast.261, f32[2,1024,1024,2]{2,1,3,0:T(8,128)} %copy-done.1, f32[2,2,1024]{2,1,0:T(2,128)S(1)} %log_add_fusion, pred[1024,1024]{0,1:T(8,128)(4,1)S(1)} %broadcast_compare_fusion), kind=kOutput, calls=%fused_computation.65 | convolution fusion | flops 1090781184 | bytes 19415040 | tf_op jit(solution)/shard_map/kgrt,rkgd->tkd/dot_general | solution.py:156
  305.8 12.4 %fusion = (f32[2,2,1024]{2,1,0:T(2,128)S(1)}, f32[2,1024,1024,2]{2,1,3,0:T(8,128)}) fusion(f32[2,1024,1024,2]{2,1,3,0:T(8,128)} %copy-done.1, f32[2,2,1024]{2,1,0:T(2,128)S(1)} %log_add_fusion, pred[1024,1024]{0,1:T(8,128)(4,1)S(1)} %broadcast_compare_fusion, bf16[1024,2,128,1]{0,2,3,1:T(8,128)(2,1)S(1)} %bitcast.264, bf16[1024,2,2,128]{0,3,2,1:T(8,128)(2,1)S(1)} %bitcast.262), kind=kOutput, calls=%fused_computation.2 | convolution fusion | flops 1094709248 | bytes 36208640 | tf_op jit(solution)/shard_map/rkgd,tkd->kgrt/dot_general | solution.py:155
  318.2 12.4 %fusion.2 = bf16[2,2,1024,1024]{2,3,1,0:T(8,128)(2,1)S(1)} fusion(f32[2,1024,1024,2]{2,1,3,0:T(8,128)} %get-tuple-element.84, f32[2,1024,1024,2]{2,1,3,0:T(8,128)} %copy-done.1, f32[2,2,1024]{2,1,0:T(2,128)S(1)} %get-tuple-element.83, f32[2,2,1024]{2,1,0:T(2,128)S(1)} %log_add_fusion, pred[1024,1024]{0,1:T(8,128)(4,1)S(1)} %broadcast_compare_fusion), kind=kLoop, calls=%fused_computation.4 | loop fusion | flops 25165824 | bytes 43024384 | tf_op jit(solution)/shard_map/convert_element_type | solution.py:160
  354.6 3.9 add_convert_fusion
  358.5 4.5 convolution_convert_fusion.1
  363.1 247.1 %all-reduce.8.cloned.1.call-done = (bf16[4,256,512]{2,1,0:T(8,128)(2,1)}, bf16[4,256,256]{2,1,0:T(8,128)(2,1)}, bf16[4,256,256]{2,1,0:T(8,128)(2,1)}, bf16[512,1...) async-done(((bf16[4,256,512]{2,1,0:T(8,128)(2,1)}, bf16[4,256,256]{2,1,0:T(8,128)(2,1)}, ...) | async-done | bytes 7864336 | tf_op jit(solution)/shard_map/psum | solution.py:180
  610.2 13.2 %all_to_all.160 = bf16[4,256,256]{2,1,0:T(8,128)(2,1)} all-to-all(bf16[4,256,256]{2,1,0:T(8,128)(2,1)} %get-tuple-element.34), channel_id=1, replica_groups=mesh['shard'=4,'replica'=8] {'shard'}, dimensions={0} | all-to-all | bytes 1048576 | tf_op jit(solution)/shard_map/all_to_all | solution.py:58
  623.4 18.6 %all_to_all.161 = bf16[4,256,256]{2,1,0:T(8,128)(2,1)} all-to-all(bf16[4,256,256]{2,1,0:T(8,128)(2,1)} %get-tuple-element.35), channel_id=1, replica_groups=mesh['shard'=4,'replica'=8] {'shard'}, dimensions={0} | all-to-all | bytes 1048576 | tf_op jit(solution)/shard_map/all_to_all | solution.py:58
  642.0 17.6 %all_to_all.162 = bf16[4,256,512]{2,1,0:T(8,128)(2,1)} all-to-all(bf16[4,256,512]{2,1,0:T(8,128)(2,1)S(1)} %copy-done.34), channel_id=1, replica_groups=mesh['shard'=4,'replica'=8] {'shard'}, dimensions={0} | all-to-all | bytes 2097152 | tf_op jit(solution)/shard_map/all_to_all | solution.py:58
  659.6 4.5 all-to-all-start.9
  665.7 62.1 %psum.56 = f32[2304]{0:T(1024)S(1)} all-reduce(f32[2304]{0:T(1024)S(1)} %pad_maximum_fusion.1), channel_id=1, replica_groups=mesh['shard'=4,'replica'=8] {'shard','replica'}, use_global_device_ids=true, to_apply=%region_19.20 | all-reduce | flops 2304 | bytes 18432 | tf_op jit(solution)/shard_map/psum | solution.py:190
  749.1 6.4 all-to-all-done.8
  (231 shorter events, 128.6 us)
Async XLA Ops:
  7.2 215.3 %copy-start = (bf16[768,1024]{1,0:T(8,128)(2,1)S(1)}, bf16[768,1024]{1,0:T(8,128)(2,1)}, u32[]{:S(2)}) copy-start(bf16[768,1024]{1,0:T(8,128)(2,1)} %param.31) | copy-start | bytes 4718596
  7.2 15.0 %copy-start.39 = (bf16[256,1024]{1,0:T(8,128)(2,1)S(1)}, bf16[256,1024]{1,0:T(8,128)(2,1)}, u32[]{:S(2)}) copy-start(bf16[256,1024]{1,0:T(8,128)(2,1)} %param.23) | copy-start | bytes 1572868
  7.2 66.6 %all-gather.6.cloned.1.call-start = ((), (), s32[]{:S(2)}) async-start(), calls=%async_computation.14 | async-start | bytes 2621440 | tf_op jit(solution)/shard_map/all_gather | solution.py:46
  23.4 15.9 %all-to-all-start.1 = ((bf16[256,4,256]{2,0,1:T(8,128)(2,1)}), bf16[256,4,256]{2,0,1:T(8,128)(2,1)S(1)}, u32[]{:S(2)}, u32[]{:S(2)}) async-start(bf16[256,4,256]{2,0,1:T(8,128)(2,1)} %copy.103), calls=%async_computation.1 | async-start | bytes 1048576 | tf_op jit(solution)/shard_map/all_to_all | solution.py:54
  39.3 7.2 copy-start.13
  39.3 13.4 %all-to-all-start = ((bf16[256,4,256]{0,2,1:T(8,128)(2,1)}), bf16[256,4,256]{0,2,1:T(8,128)(2,1)}, u32[]{:S(2)}, u32[]{:S(2)}) async-start(bf16[256,4,256]{0,2,1:T(8,128)(2,1)} %bitcast.17), calls=%async_computation | async-start | bytes 1048576 | tf_op jit(solution)/shard_map/all_to_all | solution.py:54
  52.7 18.8 %all-to-all-start.2 = ((bf16[256,4,512]{2,0,1:T(8,128)(2,1)}), bf16[256,4,512]{2,0,1:T(8,128)(2,1)}, u32[]{:S(2)}, u32[]{:S(2)}) async-start(bf16[256,4,512]{2,0,1:T(8,128)(2,1)} %copy.106), calls=%async_computation.2 | async-start | bytes 2097152 | tf_op jit(solution)/shard_map/all_to_all | solution.py:54
  57.0 76.9 %reduce-scatter.5.cloned.1.call-start = ((), (), s32[]{:S(2)}) async-start(), calls=%async_computation.15 | async-start | bytes 2621440 | tf_op jit(solution)/shard_map/reduce_scatter | solution.py:50
  60.2 21.9 %copy-start.8 = (f32[1024,128]{0,1:T(8,128)}, f32[1024,128]{0,1:T(8,128)S(1)}, u32[]{:S(2)}) copy-start(f32[1024,128]{0,1:T(8,128)S(1)} %get-tuple-element.60) | copy-start | bytes 1572868
  86.3 5.8 copy-start.1
  90.8 7.3 copy-start.36
  92.0 6.1 copy-start.48
  102.0 31.9 %copy-start.4 = (bf16[1,256,1024]{2,1,0:T(8,128)(2,1)S(1)}, bf16[1,256,1024]{2,1,0:T(8,128)(2,1)}, u32[]{:S(2)}) copy-start(bf16[1,256,1024]{2,1,0:T(8,128)(2,1)} %param.17) | copy-start | bytes 1572868
  102.0 111.4 %all-gather.8.cloned.1.call-start = ((), (), s32[]{:S(2)}) async-start(), calls=%async_computation.16 | async-start | bytes 2621440 | tf_op jit(solution)/shard_map/all_gather | solution.py:46
  139.8 35.6 %all-to-all-start.3 = ((bf16[256,4,768]{0,2,1:T(8,128)(2,1)}), bf16[256,4,768]{0,2,1:T(8,128)(2,1)}, u32[]{:S(2)}, u32[]{:S(2)}) async-start(bf16[256,4,768]{0,2,1:T(8,128)(2,1)} %bitcast.234), calls=%async_computation.4 | async-start | bytes 3145728 | tf_op jit(solution)/shard_map/all_to_all | solution.py:54
  144.2 78.3 %all-gather.10.cloned.1.call-start = ((), (), s32[]{:S(2)}) async-start(), calls=%async_computation.18 | async-start | bytes 2621440 | tf_op jit(solution)/shard_map/all_gather | solution.py:46
  175.4 35.4 %all-to-all-start.4 = ((bf16[256,4,768]{0,2,1:T(8,128)(2,1)}), bf16[256,4,768]{0,2,1:T(8,128)(2,1)}, u32[]{:S(2)}, u32[]{:S(2)}) async-start(bf16[256,4,768]{0,2,1:T(8,128)(2,1)} %bitcast.235), calls=%async_computation.5 | async-start | bytes 3145728 | tf_op jit(solution)/shard_map/all_to_all | solution.py:54
  179.8 87.2 %reduce-scatter.9.cloned.1.call-start = ((), (), s32[]{:S(2)}) async-start(), calls=%async_computation.19 | async-start | bytes 2621440 | tf_op jit(solution)/shard_map/reduce_scatter | solution.py:50
  222.5 7.2 copy-start.31
  235.4 58.6 %all-gather.12.cloned.1.call-start = ((), (), s32[]{:S(2)}) async-start(), calls=%async_computation.20 | async-start | bytes 2621440 | tf_op jit(solution)/shard_map/all_gather | solution.py:46
  271.3 338.9 %all-reduce.8.cloned.1.call-start = ((), (), s32[]{:S(2)}) async-start(), calls=%async_computation.22 | async-start | bytes 15728640 | tf_op jit(solution)/shard_map/psum | solution.py:180
  297.2 8.5 %copy-start.37 = (bf16[1024,256]{0,1:T(8,128)(2,1)S(1)}, bf16[1024,256]{0,1:T(8,128)(2,1)}, u32[]{:S(2)}) copy-start(bf16[1024,256]{0,1:T(8,128)(2,1)} %copy-done.36) | copy-start | bytes 1572868
  305.8 39.2 %copy-start.38 = (bf16[2,128,1024]{2,1,0:T(8,128)(2,1)}, bf16[2,128,1024]{2,1,0:T(8,128)(2,1)S(1)}, u32[]{:S(2)}) copy-start(bf16[2,128,1024]{2,1,0:T(8,128)(2,1)S(1)} %fusion.18) | copy-start | bytes 1572868
  318.2 12.4 %copy-start.29 = (bf16[1024,2,128,1]{0,2,3,1:T(8,128)(2,1)S(1)}, bf16[1024,2,128,1]{0,2,3,1:T(8,128)(2,1)}, u32[]{:S(2)}) copy-start(bf16[1024,2,128,1]{0,2,3,1:T(8,128)(2,1)} %copy-done.28) | copy-start | bytes 1572868
  340.6 5.9 copy-start.25
  350.4 313.7 %reduce-scatter.11.cloned.1.call-start = ((), (), s32[]{:S(2)}) async-start(), calls=%async_computation.21 | async-start | bytes 2621440 | tf_op jit(solution)/shard_map/reduce_scatter | solution.py:50
  358.5 370.0 %reduce-scatter.7.cloned.1.call-start = ((), (), s32[]{:S(2)}) async-start(), calls=%async_computation.17 | async-start | bytes 2621440 | tf_op jit(solution)/shard_map/reduce_scatter | solution.py:50
  610.2 31.7 %copy-start.34 = (bf16[4,256,512]{2,1,0:T(8,128)(2,1)S(1)}, bf16[4,256,512]{2,1,0:T(8,128)(2,1)}, u32[]{:S(2)}) copy-start(bf16[4,256,512]{2,1,0:T(8,128)(2,1)} %get-tuple-element.33) | copy-start | bytes 3145732
  659.6 68.9 %copy-start.7 = (bf16[256,1024]{1,0:T(8,128)(2,1)S(1)}, bf16[256,1024]{1,0:T(8,128)(2,1)}, u32[]{:S(2)}) copy-start(bf16[256,1024]{1,0:T(8,128)(2,1)} %reduce-scatter.5.cloned.1.call-done) | copy-start | bytes 1572868
  659.6 68.9 %copy-start.12 = (bf16[1,256,1024]{2,1,0:T(8,128)(2,1)S(1)}, bf16[1,256,1024]{2,1,0:T(8,128)(2,1)}, u32[]{:S(2)}) copy-start(bf16[1,256,1024]{2,1,0:T(8,128)(2,1)} %param.18) | copy-start | bytes 1572868
  659.6 72.2 %all-to-all-start.9 = ((bf16[4,256,768]{2,1,0:T(8,128)(2,1)}), bf16[4,256,768]{2,1,0:T(8,128)(2,1)}, u32[]{:S(2)}, u32[]{:S(2)}) async-start(bf16[4,256,768]{2,1,0:T(8,128)(2,1)} %get-tuple-element.38), calls=%async_computation.13 | async-start | bytes 3145728 | tf_op jit(solution)/shard_map/all_to_all | solution.py:58
  731.9 23.7 %all-to-all-start.8 = ((bf16[4,256,768]{2,1,0:T(8,128)(2,1)}), bf16[4,256,768]{2,1,0:T(8,128)(2,1)S(1)}, u32[]{:S(2)}, u32[]{:S(2)}) async-start(bf16[4,256,768]{2,1,0:T(8,128)(2,1)} %get-tuple-element.37), calls=%async_computation.12 | async-start | bytes 3145728 | tf_op jit(solution)/shard_map/all_to_all | solution.py:58
  (38 other events, 100.4 us)
Sparse Core Ops, SparseCore 0:
  22.3 26.2 all-gather.5
  102.1 31.7 reduce-scatter.4
  137.4 33.7 all-gather.7
  172.7 33.7 all-gather.9
  235.6 31.4 reduce-scatter.8
  271.5 22.5 all-gather.11
  350.6 259.6 all-reduce.7
  613.3 35.3 reduce-scatter.10
  652.0 42.2 reduce-scatter.6
where the time goes:
time: 769 us; the launch traced here: 765 us
  waiting for transfers between devices  400 us (52%)
  blocking collectives  120 us (16%)
  matrix products  97.4 us (13%)
  other arithmetic  56.2 us (7%)
  local copies, waits for them, and re-layouts  44.7 us (6%)
  starting transfers between devices  29.9 us (4%)
  between operations  16.3 us (2%)
    psum x1, waiting for transfers between devices, total(): return lax.psum(v.astype(BF), 'replica').astype(F32)  247 us
    all_to_all x5, waiting for transfers between devices, to_columns(): return lax.all_to_all(w, 'shard', split_axis=1, concat_axis=0, tiled=True)  72.1 us
    reduce_scatter x4, waiting for transfers between devices, scatter_rows(): lax.psum_scatter(v.astype(BF), 'shard', scatter_dimension=0, tiled=True)  63.4 us
    psum x1, blocking collectives, shards(): small = lax.psum(small, ('shard', 'replica'))  62.1 us
    all_to_all x3, blocking collectives, to_rows(): return lax.all_to_all(g, 'shard', split_axis=0, concat_axis=1, tiled=True)  49.4 us
    dot_general x7, matrix products, mm(): return jnp.einsum('ri,io->ro', a, b, preferred_element_type=F32)  22 us
    dot_general x7, matrix products, mm_t(): return jnp.einsum('ro,io->ri', a, b, preferred_element_type=F32)  21.9 us
    all_to_all x5, starting transfers between devices, to_columns(): return lax.all_to_all(w, 'shard', split_axis=1, concat_axis=0, tiled=True)  20.6 us
  transfers between devices with their start and end apart: 16, of which 10 were waited for; matrix products, arithmetic and copies ran while one was open for 11% of the time, Pallas kernels for 0%

commit v1 on v0

--- a/solution.py
+++ b/solution.py
@@ -55,7 +55,10 @@
 
 
 def to_rows(g):
-    return lax.all_to_all(g, "shard", split_axis=0, concat_axis=1, tiled=True)
+    return jnp.concatenate(
+        lax.all_to_all(jnp.stack(jnp.split(g, lax.axis_size("shard"), axis=0)), "shard", 0, 0),
+        axis=1,
+    )
 
 
 def shards(

time: 769 us -> 797 us (1.036)
  blocking collectives: 120 us -> 68.8 us
  local copies, waits for them, and re-layouts: 44.7 us -> 70.8 us
  waiting for transfers between devices: 400 us -> 424 us
  other arithmetic: 56.2 us -> 72.5 us
  starting transfers between devices: 29.9 us -> 42.1 us
    all_to_all x3 -> x0, blocking collectives: 49.4 us -> none  [to_rows(): return lax.all_to_all(g, 'shard', split_axis=0, concat_axis=1, tiled=True)]
    all_to_all x2 -> x5, waiting for transfers between devices: 6.45 us -> 30.2 us  [to_rows(): lax.all_to_all(jnp.stack(jnp.split(g, lax.axis_size('shard'), axis=0)), '...]
    unnamed x118 -> x141, local copies, waits for them, and re-layouts: 20.5 us -> 35 us
    all_to_all x2 -> x5, starting transfers between devices: 8.1 us -> 20.3 us  [to_rows(): lax.all_to_all(jnp.stack(jnp.split(g, lax.axis_size('shard'), axis=0)), '...]
    convert_element_type x0 -> x5, other arithmetic: none -> 9.67 us  [the longest x1 3.34 us: shards(): to_rows(total(mm_w(normed2, grad_gate)).astype(BF)).astype(F32)]
  transfers between devices with their start and end apart: 16 -> 19, of which waited for: 10 -> 12; matrix products, arithmetic and copies ran while one was open for 11% -> 15% of each run, Pallas kernels for 0% -> 0%
where the time goes in v1:
time: 797 us; the launch traced here: 792 us
  waiting for transfers between devices  424 us (53%)
  matrix products  97.5 us (12%)
  other arithmetic  72.5 us (9%)
  local copies, waits for them, and re-layouts  70.8 us (9%)
  blocking collectives  68.8 us (9%)
  starting transfers between devices  42.1 us (5%)
  between operations  16.4 us (2%)
    psum x1, waiting for transfers between devices, total(): return lax.psum(v.astype(BF), 'replica').astype(F32)  247 us
    all_to_all x5, waiting for transfers between devices, to_columns(): return lax.all_to_all(w, 'shard', split_axis=1, concat_axis=0, tiled=True)  72.2 us
    reduce_scatter x4, waiting for transfers between devices, scatter_rows(): lax.psum_scatter(v.astype(BF), 'shard', scatter_dimension=0, tiled=True)  63.4 us
    psum x1, blocking collectives, shards(): small = lax.psum(small, ('shard', 'replica'))  60.3 us
    unnamed x141, local copies, waits for them, and re-layouts  35 us
    all_to_all x5, waiting for transfers between devices, to_rows(): lax.all_to_all(jnp.stack(jnp.split(g, lax.axis_size('shard'), axis=0)), '...  30.2 us
    dot_general x7, matrix products, mm(): return jnp.einsum('ri,io->ro', a, b, preferred_element_type=F32)  22 us
    dot_general x7, matrix products, mm_t(): return jnp.einsum('ro,io->ri', a, b, preferred_element_type=F32)  21.9 us
  transfers between devices with their start and end apart: 19, of which 12 were waited for; matrix products, arithmetic and copies ran while one was open for 15% of the time, Pallas kernels for 0%

profile of v1, /device:TPU:0, one launch (start us, length us, event | category | flops | bytes accessed | tf_op | source)
XLA Modules:
  0.0 792.2 jit_solution(4842083265763630549)
XLA Ops:
  11.6 8.5 %all-reduce.4 = bf16[2304]{0:T(1024)(128)(2,1)S(1)} all-reduce(bf16[2304]{0:T(1024)(128)(2,1)S(1)} %dynamic-update-slice.3), channel_id=2, replica_groups=mesh['shard'=4,'replica'=8] {'shard'}, use_global_device_ids=true, to_apply=%add.4 | all-reduce | flops 2304 | bytes 9216
  28.6 4.6 compare_select_fusion.1
  33.2 6.2 all-to-all-done.1
  39.4 4.2 all-to-all-start
  47.3 5.5 all-to-all-done
  52.7 4.2 all-to-all-start.2
  64.9 6.6 all-to-all-done.2
  92.1 6.1 convolution_convert_fusion.8
  98.2 3.9 convolution_convert_fusion
  102.1 31.8 %reduce-scatter.5.cloned.1.call-done = bf16[256,1024]{1,0:T(8,128)(2,1)} async-done(((bf16[1024,1024]{1,0:T(8,128)(2,1)}), bf16[256,1024]{1,0:T(8,128)(2,1)}) %reduce-scatter.5.cloned.1.call-update) | async-done | bytes 524304 | tf_op jit(solution)/shard_map/reduce_scatter | solution.py:50
  139.9 4.4 all-to-all-start.3
  149.7 25.8 %all-to-all-done.3 = bf16[256,4,768]{0,2,1:T(8,128)(2,1)} async-done(((bf16[256,4,768]{0,2,1:T(8,128)(2,1)}), bf16[256,4,768]{0,2,1:T(8,128)(2,1)}, u32[]{:S(2)}, u32[]{:S(2)}) %all-to-all-start.3) | async-done | bytes 1572896 | tf_op jit(solution)/shard_map/all_to_all | solution.py:54
  175.5 4.4 all-to-all-start.4
  182.8 28.1 %all-to-all-done.4 = bf16[256,4,768]{0,2,1:T(8,128)(2,1)} async-done(((bf16[256,4,768]{0,2,1:T(8,128)(2,1)}), bf16[256,4,768]{0,2,1:T(8,128)(2,1)}, u32[]{:S(2)}, u32[]{:S(2)}) %all-to-all-start.4) | async-done | bytes 1572896 | tf_op jit(solution)/shard_map/all_to_all | solution.py:54
  213.4 5.6 fusion.63
  222.5 7.3 multiply_convert_fusion
  235.6 31.5 %reduce-scatter.9.cloned.1.call-done = bf16[256,1024]{1,0:T(8,128)(2,1)} async-done(((bf16[1024,1024]{1,0:T(8,128)(2,1)}), bf16[256,1024]{1,0:T(8,128)(2,1)}) %reduce-scatter.9.cloned.1.call-update) | async-done | bytes 524304 | tf_op jit(solution)/shard_map/reduce_scatter | solution.py:50
  272.5 5.2 convolution_convert_fusion.3
  283.8 11.0 %all-gather.12.cloned.1.call-done = bf16[1024,1024]{1,0:T(8,128)(2,1)} async-done(((bf16[256,1024]{1,0:T(8,128)(2,1)}), bf16[1024,1024]{1,0:T(8,128)(2,1)}) %all-gather.12.cloned.1.call-update) | async-done | bytes 2097168 | tf_op jit(solution)/shard_map/all_gather | solution.py:46
  297.9 8.5 %fusion.18 = bf16[2,128,1024]{2,1,0:T(8,128)(2,1)S(1)} fusion(bf16[1024,2,2,128]{0,3,2,1:T(8,128)(2,1)S(1)} %bitcast.288, f32[2,1024,1024,2]{2,1,3,0:T(8,128)} %copy-done.1, f32[2,2,1024]{2,1,0:T(2,128)S(1)} %log_add_fusion, pred[1024,1024]{0,1:T(8,128)(4,1)S(1)} %broadcast_compare_fusion), kind=kOutput, calls=%fused_computation.67 | convolution fusion | flops 1090781184 | bytes 19415040 | tf_op jit(solution)/shard_map/kgrt,rkgd->tkd/dot_general | solution.py:159
  306.5 12.5 %fusion = (f32[2,2,1024]{2,1,0:T(2,128)S(1)}, f32[2,1024,1024,2]{2,1,3,0:T(8,128)}) fusion(f32[2,1024,1024,2]{2,1,3,0:T(8,128)} %copy-done.1, f32[2,2,1024]{2,1,0:T(2,128)S(1)} %log_add_fusion, pred[1024,1024]{0,1:T(8,128)(4,1)S(1)} %broadcast_compare_fusion, bf16[1024,2,128,1]{0,2,3,1:T(8,128)(2,1)S(1)} %bitcast.291, bf16[1024,2,2,128]{0,3,2,1:T(8,128)(2,1)S(1)} %bitcast.289), kind=kOutput, calls=%fused_computation.2 | convolution fusion | flops 1094709248 | bytes 36208640 | tf_op jit(solution)/shard_map/rkgd,tkd->kgrt/dot_general | solution.py:158
  318.9 12.4 %fusion.2 = bf16[2,2,1024,1024]{2,3,1,0:T(8,128)(2,1)S(1)} fusion(f32[2,1024,1024,2]{2,1,3,0:T(8,128)} %get-tuple-element.156, f32[2,1024,1024,2]{2,1,3,0:T(8,128)} %copy-done.1, f32[2,2,1024]{2,1,0:T(2,128)S(1)} %get-tuple-element.155, f32[2,2,1024]{2,1,0:T(2,128)S(1)} %log_add_fusion, pred[1024,1024]{0,1:T(8,128)(4,1)S(1)} %broadcast_compare_fusion), kind=kLoop, calls=%fused_computation.4 | loop fusion | flops 25165824 | bytes 43024384 | tf_op jit(solution)/shard_map/convert_element_type | solution.py:163
  355.7 3.9 add_convert_fusion
  359.7 4.5 convolution_convert_fusion.1
  364.2 247.1 %all-reduce.8.cloned.1.call-done = (bf16[1024,512]{1,0:T(8,128)(2,1)}, bf16[1024,256]{1,0:T(8,128)(2,1)}, bf16[1024,256]{1,0:T(8,128)(2,1)}, bf16[512,1024]{1,0:...) async-done(((bf16[1024,512]{1,0:T(8,128)(2,1)}, bf16[1024,256]{1,0:T(8,128)(2,1)}, bf16[1024,256]{1,0:T(8,128)(2,1)}, ...) | async-done | bytes 7864336 | tf_op jit(solution)/shard_map/psum | solution.py:183
  617.9 7.9 %all-to-all-done.7 = bf16[4,256,256]{2,1,0:T(8,128)(2,1)S(1)} async-done(((bf16[4,256,256]{2,1,0:T(8,128)(2,1)}), bf16[4,256,256]{2,1,0:T(8,128)(2,1)S(1)}, u32[]{:S(2)}, u32[]{:S(2)}) %all-to-all-start.7) | async-done | bytes 524320 | tf_op jit(solution)/shard_map/all_to_all | solution.py:59
  631.8 12.0 %all-to-all-done.6 = bf16[4,256,256]{2,1,0:T(8,128)(2,1)S(1)} async-done(((bf16[4,256,256]{2,1,0:T(8,128)(2,1)}), bf16[4,256,256]{2,1,0:T(8,128)(2,1)S(1)}, u32[]{:S(2)}, u32[]{:S(2)}) %all-to-all-start.6) | async-done | bytes 524320 | tf_op jit(solution)/shard_map/all_to_all | solution.py:59
  643.8 4.3 all-to-all-start.5
  652.4 10.2 %all-to-all-done.5 = bf16[4,256,512]{2,1,0:T(8,128)(2,1)} async-done(((bf16[4,256,512]{2,1,0:T(8,128)(2,1)}), bf16[4,256,512]{2,1,0:T(8,128)(2,1)}, u32[]{:S(2)}, u32[]{:S(2)}) %all-to-all-start.5) | async-done | bytes 1048608 | tf_op jit(solution)/shard_map/all_to_all | solution.py:59
  662.6 4.4 all-to-all-start.9
  670.4 60.3 %psum.56 = f32[2304]{0:T(1024)} all-reduce(f32[2304]{0:T(1024)} %pad_maximum_fusion.6), channel_id=1, replica_groups=mesh['shard'=4,'replica'=8] {'shard','replica'}, use_global_device_ids=true, to_apply=%region_19.20 | all-reduce | flops 2304 | bytes 18432 | tf_op jit(solution)/shard_map/psum | solution.py:193
  738.2 4.8 all-to-all-start.8
  (265 shorter events, 178.2 us)
Async XLA Ops:
  7.2 215.4 %copy-start = (bf16[768,1024]{1,0:T(8,128)(2,1)S(1)}, bf16[768,1024]{1,0:T(8,128)(2,1)}, u32[]{:S(2)}) copy-start(bf16[768,1024]{1,0:T(8,128)(2,1)} %param.31) | copy-start | bytes 4718596
  7.2 15.1 %copy-start.43 = (bf16[256,1024]{1,0:T(8,128)(2,1)S(1)}, bf16[256,1024]{1,0:T(8,128)(2,1)}, u32[]{:S(2)}) copy-start(bf16[256,1024]{1,0:T(8,128)(2,1)} %param.23) | copy-start | bytes 1572868
  7.2 66.6 %all-gather.6.cloned.1.call-start = ((), (), s32[]{:S(2)}) async-start(), calls=%async_computation.14 | async-start | bytes 2621440 | tf_op jit(solution)/shard_map/all_gather | solution.py:46
  8.7 14.8 %copy-start.48 = (f32[256]{0:T(256)}, f32[256]{0:T(256)S(1)}, u32[]{:S(2)}) copy-start(f32[256]{0:T(256)S(1)} %fusion.49) | copy-start | bytes 3076
  23.5 15.9 %all-to-all-start.1 = ((bf16[256,4,256]{2,0,1:T(8,128)(2,1)}), bf16[256,4,256]{2,0,1:T(8,128)(2,1)S(1)}, u32[]{:S(2)}, u32[]{:S(2)}) async-start(bf16[256,4,256]{2,0,1:T(8,128)(2,1)} %copy.113), calls=%async_computation.1 | async-start | bytes 1048576 | tf_op jit(solution)/shard_map/all_to_all | solution.py:54
  39.4 13.4 %all-to-all-start = ((bf16[256,4,256]{0,2,1:T(8,128)(2,1)}), bf16[256,4,256]{0,2,1:T(8,128)(2,1)}, u32[]{:S(2)}, u32[]{:S(2)}) async-start(bf16[256,4,256]{0,2,1:T(8,128)(2,1)} %bitcast.17), calls=%async_computation | async-start | bytes 1048576 | tf_op jit(solution)/shard_map/all_to_all | solution.py:54
  52.7 18.8 %all-to-all-start.2 = ((bf16[256,4,512]{2,0,1:T(8,128)(2,1)}), bf16[256,4,512]{2,0,1:T(8,128)(2,1)}, u32[]{:S(2)}, u32[]{:S(2)}) async-start(bf16[256,4,512]{2,0,1:T(8,128)(2,1)} %copy.116), calls=%async_computation.2 | async-start | bytes 2097152 | tf_op jit(solution)/shard_map/all_to_all | solution.py:54
  57.0 77.0 %reduce-scatter.5.cloned.1.call-start = ((), (), s32[]{:S(2)}) async-start(), calls=%async_computation.15 | async-start | bytes 2621440 | tf_op jit(solution)/shard_map/reduce_scatter | solution.py:50
  60.1 21.9 %copy-start.8 = (f32[1024,128]{0,1:T(8,128)}, f32[1024,128]{0,1:T(8,128)S(1)}, u32[]{:S(2)}) copy-start(f32[1024,128]{0,1:T(8,128)S(1)} %get-tuple-element.132) | copy-start | bytes 1572868
  90.8 7.4 copy-start.40
  102.1 31.9 %copy-start.4 = (bf16[1,256,1024]{2,1,0:T(8,128)(2,1)S(1)}, bf16[1,256,1024]{2,1,0:T(8,128)(2,1)}, u32[]{:S(2)}) copy-start(bf16[1,256,1024]{2,1,0:T(8,128)(2,1)} %param.17) | copy-start | bytes 1572868
  102.1 111.3 %all-gather.8.cloned.1.call-start = ((), (), s32[]{:S(2)}) async-start(), calls=%async_computation.16 | async-start | bytes 2621440 | tf_op jit(solution)/shard_map/all_gather | solution.py:46
  139.9 35.6 %all-to-all-start.3 = ((bf16[256,4,768]{0,2,1:T(8,128)(2,1)}), bf16[256,4,768]{0,2,1:T(8,128)(2,1)}, u32[]{:S(2)}, u32[]{:S(2)}) async-start(bf16[256,4,768]{0,2,1:T(8,128)(2,1)} %bitcast.267), calls=%async_computation.4 | async-start | bytes 3145728 | tf_op jit(solution)/shard_map/all_to_all | solution.py:54
  144.3 78.3 %all-gather.10.cloned.1.call-start = ((), (), s32[]{:S(2)}) async-start(), calls=%async_computation.18 | async-start | bytes 2621440 | tf_op jit(solution)/shard_map/all_gather | solution.py:46
  175.5 35.3 %all-to-all-start.4 = ((bf16[256,4,768]{0,2,1:T(8,128)(2,1)}), bf16[256,4,768]{0,2,1:T(8,128)(2,1)}, u32[]{:S(2)}, u32[]{:S(2)}) async-start(bf16[256,4,768]{0,2,1:T(8,128)(2,1)} %bitcast.268), calls=%async_computation.5 | async-start | bytes 3145728 | tf_op jit(solution)/shard_map/all_to_all | solution.py:54
  179.9 87.3 %reduce-scatter.9.cloned.1.call-start = ((), (), s32[]{:S(2)}) async-start(), calls=%async_computation.19 | async-start | bytes 2621440 | tf_op jit(solution)/shard_map/reduce_scatter | solution.py:50
  235.5 59.2 %all-gather.12.cloned.1.call-start = ((), (), s32[]{:S(2)}) async-start(), calls=%async_computation.20 | async-start | bytes 2621440 | tf_op jit(solution)/shard_map/all_gather | solution.py:46
  269.4 8.3 %copy-start.49 = (f32[256]{0:T(256)}, f32[256]{0:T(256)S(1)}, u32[]{:S(2)}) copy-start(f32[256]{0:T(256)S(1)} %multiply_multiply_fusion.5) | copy-start | bytes 3076
  272.0 339.3 %all-reduce.8.cloned.1.call-start = ((), (), s32[]{:S(2)}) async-start(), calls=%async_computation.22 | async-start | bytes 15728640 | tf_op jit(solution)/shard_map/psum | solution.py:183
  297.9 8.5 %copy-start.41 = (bf16[1024,256]{0,1:T(8,128)(2,1)S(1)}, bf16[1024,256]{0,1:T(8,128)(2,1)}, u32[]{:S(2)}) copy-start(bf16[1024,256]{0,1:T(8,128)(2,1)} %copy-done.40) | copy-start | bytes 1572868
  306.4 39.7 %copy-start.42 = (bf16[2,128,1024]{2,1,0:T(8,128)(2,1)}, bf16[2,128,1024]{2,1,0:T(8,128)(2,1)S(1)}, u32[]{:S(2)}) copy-start(bf16[2,128,1024]{2,1,0:T(8,128)(2,1)S(1)} %fusion.18) | copy-start | bytes 1572868
  318.9 12.4 %copy-start.30 = (bf16[1024,2,128,1]{0,2,3,1:T(8,128)(2,1)S(1)}, bf16[1024,2,128,1]{0,2,3,1:T(8,128)(2,1)}, u32[]{:S(2)}) copy-start(bf16[1024,2,128,1]{0,2,3,1:T(8,128)(2,1)} %copy-done.29) | copy-start | bytes 1572868
  351.6 315.4 %reduce-scatter.11.cloned.1.call-start = ((), (), s32[]{:S(2)}) async-start(), calls=%async_computation.21 | async-start | bytes 2621440 | tf_op jit(solution)/shard_map/reduce_scatter | solution.py:50
  359.6 373.7 %reduce-scatter.7.cloned.1.call-start = ((), (), s32[]{:S(2)}) async-start(), calls=%async_computation.17 | async-start | bytes 2621440 | tf_op jit(solution)/shard_map/reduce_scatter | solution.py:50
  613.6 12.3 %all-to-all-start.7 = ((bf16[4,256,256]{2,1,0:T(8,128)(2,1)}), bf16[4,256,256]{2,1,0:T(8,128)(2,1)S(1)}, u32[]{:S(2)}, u32[]{:S(2)}) async-start(bf16[4,256,256]{2,1,0:T(8,128)(2,1)} %pad_maximum_fusion.5), calls=%async_computation.11 | async-start | bytes 1048576 | tf_op jit(solution)/shard_map/all_to_all | solution.py:59
  625.9 17.9 %all-to-all-start.6 = ((bf16[4,256,256]{2,1,0:T(8,128)(2,1)}), bf16[4,256,256]{2,1,0:T(8,128)(2,1)S(1)}, u32[]{:S(2)}, u32[]{:S(2)}) async-start(bf16[4,256,256]{2,1,0:T(8,128)(2,1)} %pad_maximum_fusion.4), calls=%async_computation.10 | async-start | bytes 1048576 | tf_op jit(solution)/shard_map/all_to_all | solution.py:59
  643.8 18.8 %all-to-all-start.5 = ((bf16[4,256,512]{2,1,0:T(8,128)(2,1)}), bf16[4,256,512]{2,1,0:T(8,128)(2,1)}, u32[]{:S(2)}, u32[]{:S(2)}) async-start(bf16[4,256,512]{2,1,0:T(8,128)(2,1)} %pad_maximum_fusion.2), calls=%async_computation.9 | async-start | bytes 2097152 | tf_op jit(solution)/shard_map/all_to_all | solution.py:59
  652.4 14.6 %copy-start.46 = (f32[1,2,4,128]{3,1,2,0:T(2,128)S(1)}, f32[1,2,4,128]{3,1,2,0:T(2,128)}, u32[]{:S(2)}) copy-start(f32[1,2,4,128]{3,1,2,0:T(2,128)} %copy-done.45) | copy-start | bytes 12292
  652.4 80.9 %copy-start.7 = (bf16[256,1024]{1,0:T(8,128)(2,1)S(1)}, bf16[256,1024]{1,0:T(8,128)(2,1)}, u32[]{:S(2)}) copy-start(bf16[256,1024]{1,0:T(8,128)(2,1)} %reduce-scatter.5.cloned.1.call-done) | copy-start | bytes 1572868
  652.4 80.9 %copy-start.12 = (bf16[1,256,1024]{2,1,0:T(8,128)(2,1)S(1)}, bf16[1,256,1024]{2,1,0:T(8,128)(2,1)}, u32[]{:S(2)}) copy-start(bf16[1,256,1024]{2,1,0:T(8,128)(2,1)} %param.18) | copy-start | bytes 1572868
  662.6 75.6 %all-to-all-start.9 = ((bf16[4,256,768]{2,1,0:T(8,128)(2,1)}), bf16[4,256,768]{2,1,0:T(8,128)(2,1)}, u32[]{:S(2)}, u32[]{:S(2)}) async-start(bf16[4,256,768]{2,1,0:T(8,128)(2,1)} %pad_maximum_fusion.1), calls=%async_computation.13 | async-start | bytes 3145728 | tf_op jit(solution)/shard_map/all_to_all | solution.py:59
  738.2 36.7 %all-to-all-start.8 = ((bf16[4,256,768]{2,1,0:T(8,128)(2,1)}), bf16[4,256,768]{2,1,0:T(8,128)(2,1)}, u32[]{:S(2)}, u32[]{:S(2)}) async-start(bf16[4,256,768]{2,1,0:T(8,128)(2,1)} %pad_maximum_fusion), calls=%async_computation.12 | async-start | bytes 3145728 | tf_op jit(solution)/shard_map/all_to_all | solution.py:59
  (50 other events, 168.1 us)
Sparse Core Ops, SparseCore 0:
  22.4 26.2 all-gather.5
  102.2 31.7 reduce-scatter.4
  137.5 33.7 all-gather.7
  172.8 33.7 all-gather.9
  235.7 31.4 reduce-scatter.8
  272.1 22.5 all-gather.11
  351.7 259.6 all-reduce.7
  614.5 36.0 reduce-scatter.10
  653.8 40.6 reduce-scatter.6
